TPU v7x, 32 devices: a whole 2x2x4 slice. The times are simulated.
32 devices in a mesh: dp: 16 (over z, y, x), tensor: 2 (over core).
Axes of the slice: x: 2, y: 2, z: 4, core: 2. Of those that a mesh axis runs over, the one named last changes fastest.
Arguments:
- activations: bfloat16 [2048, 2048], P('dp', 'tensor'), may hold values from -12 to 12
- dgrad: bfloat16 [2048, 4864], P('dp', 'tensor'), may hold values from -24 to 24
- coding: int32 [16, 4], replicated, may hold values from 0 to 4, as said below
- alive: int32 [16], replicated, may hold values from 0 to 1, as said below
Outputs:
- weight_grad: float32 [2048, 4864], P('dp', 'tensor')
Inputs may be any that keep to these rules, and one draw needn't show every extreme that they name: Each entry is 0, 1, 2 or 4; coding[i, 0] is never 0; in each row the zeros come after all nonzero entries; rows 0 to 3 have no zero. Workers 0 to 3 are alive.
All inputs are finite; a program needn't handle non-finite values.
Results may differ from a plain program's by a relative error of at most 0.0003.
Values may be sent and summed in bfloat16 or wider, within the bound.
A program may use at most 128 MiB of HBM per device.

v0:
```python
import math

import jax
import jax.numpy as jnp
from jax import lax
from jax.sharding import PartitionSpec as P


def passed_along(value, axis, by):
    length = lax.axis_size(axis)
    return lax.ppermute(value, axis, [(i, (i + by) % length) for i in range(length)])


def local(activations, dgrad, coding, alive):
    workers = lax.axis_size("dp")
    position = lax.axis_index("dp")
    slots = coding.shape[1]
    rows = activations.shape[0]
    width = activations.shape[1] * lax.axis_size("tensor")
    hidden = dgrad.shape[1] * lax.axis_size("tensor")
    limit = 8.0 * math.sqrt(rows)
    overall = 1.0 / (limit * math.sqrt(workers))
    pieces = [(activations, dgrad)]
    for offset in range(1, slots):
        pieces.append(passed_along((activations, dgrad), "dp", -offset))
    coef_row = lax.dynamic_index_in_dim(coding, position, 0, keepdims=False)
    scaled_rows = jnp.concatenate(
        [pieces[offset][0] * coef_row[offset].astype(jnp.bfloat16) for offset in range(slots)],
        axis=0,
    )
    stacked_grads = jnp.concatenate([pieces[offset][1] for offset in range(slots)], axis=0)
    term = lax.dot_general(
        lax.all_gather(scaled_rows, "tensor", axis=1, tiled=True),
        stacked_grads,
        (((0,), (0,)), ((), ())),
        preferred_element_type=jnp.float32,
    )
    squares = lax.psum(jnp.sum(term * term), "tensor")
    factor = jnp.minimum(1.0, limit / jnp.sqrt(squares / (width * hidden) + 1e-06))
    present = lax.dynamic_index_in_dim(alive, position, 0, keepdims=False).astype(jnp.float32)
    return lax.psum_scatter(
        term * (present * factor * overall), "dp", scatter_dimension=0, tiled=True
    )


def solution(mesh):
    return jax.shard_map(
        local,
        mesh=mesh,
        in_specs=(P("dp", "tensor"), P("dp", "tensor"), P(), P()),
        out_specs=P("dp", "tensor"),
        check_vma=False,
    )
```

profile of v0, /device:TPU:0, one launch (start us, length us, event | category | flops | bytes accessed | tf_op | source)
XLA Modules:
  0.0 530.6 jit_solution(11652368892443571519)
XLA Ops:
  6.5 7.0 %collective-permute-start = (bf16[128,1024]{1,0:T(8,128)(2,1)}, bf16[128,1024]{1,0:T(8,128)(2,1)S(1)}, u32[]{:S(2)}, u32[]{:S(2)}) collective-permute-start(bf16[128,1024]{1,0:T(8,128)(2,1)} %param.4), channel_id=1, source_target_pairs={{0,30},{2,0},{4,2},{6,4},{8,6},{10,8},{12,10},{14,12},{16,14},{18,... | collective-permute-start | bytes 786440 | tf_op jit(solution)/shard_map/ppermute | solution.py:11
  13.5 1.0 collective-permute-start.1
  14.5 0.8 dynamic-slice_convert_fusion
  15.2 0.6 fusion.9
  15.8 1.6 broadcast_multiply_fusion.4
  17.5 4.2 collective-permute-done
  21.6 0.6 broadcast_multiply_fusion.3
  22.3 3.8 collective-permute-done.2
  26.1 0.6 broadcast_multiply_fusion.1
  26.7 3.9 collective-permute-done.1
  30.6 0.7 broadcast_multiply_fusion.2
  31.3 1.0 pad_maximum_fusion
  32.4 0.0 all-gather.2.cloned.1.call-update
  32.4 0.0 reduce-scatter.2.cloned.1.call-start
  32.4 5.1 collective-permute-start.4
  37.6 0.1 collective-permute-start.5
  37.7 0.6 dynamic_slice.9
  38.8 15.8 %collective-permute-done.4 = bf16[128,2432]{1,0:T(8,128)(2,1)S(1)} collective-permute-done((bf16[128,2432]{1,0:T(8,128)(2,1)S(1)}, bf16[128,2432]{1,0:T(8,128)(2,1)S(1)}, u32[]{:S(2)}, u32[]{:S(2)}) %collective-permute-start.4) | collective-permute-done | bytes 622624 | tf_op jit(solution)/shard_map/ppermute | solution.py:11
  54.7 14.1 %collective-permute-done.3 = bf16[128,2432]{1,0:T(8,128)(2,1)S(1)} collective-permute-done((bf16[128,2432]{1,0:T(8,128)(2,1)S(1)}, bf16[128,2432]{1,0:T(8,128)(2,1)S(1)}, u32[]{:S(2)}, u32[]{:S(2)}) %collective-permute-start.3) | collective-permute-done | bytes 622624 | tf_op jit(solution)/shard_map/ppermute | solution.py:11
  68.8 11.4 %collective-permute-done.5 = bf16[128,2432]{1,0:T(8,128)(2,1)S(1)} collective-permute-done((bf16[128,2432]{1,0:T(8,128)(2,1)S(1)}, bf16[128,2432]{1,0:T(8,128)(2,1)S(1)}, u32[]{:S(2)}, u32[]{:S(2)}) %collective-permute-start.5) | collective-permute-done | bytes 622624 | tf_op jit(solution)/shard_map/ppermute | solution.py:11
  80.2 13.9 %multiply_reduce_fusion = (f32[]{:T(128)}, f32[2048,2432]{1,0:T(8,128)}) fusion(bf16[512,2048]{1,0:T(8,128)(2,1)} %all-gather.2.cloned.1.call-done, bf16[128,2432]{1,0:T(8,128)(2,1)S(1)} %collective-permute-done.5, bf16[128,2432]{1,0:T(8,128)(2,1)S(1)} %collective-permute-done.4, bf16[128,2432]{1,0:T(8,128)(2,1)S(1)} %collective-permute-done.3, ...), kind=kOutput, calls=%fused_computation | convolution fusion | flops 5120196608 | bytes 24510468 | tf_op jit(solution)/shard_map/dot_general | solution.py:32
  94.1 3.1 psum.7
  97.9 14.9 %broadcast_multiply_fusion = f32[2048,2432]{1,0:T(8,128)} fusion(f32[2048,2432]{1,0:T(8,128)} %get-tuple-element.10, f32[]{:T(128)S(6)} %mul.49), kind=kLoop, calls=%fused_computation.1 | loop fusion | flops 4980736 | bytes 39845892 | tf_op jit(solution)/shard_map/mul | solution.py:42
  112.8 410.9 %reduce-scatter.2.cloned.1.call-done = f32[128,2432]{1,0:T(8,128)} async-done(((f32[2048,2432]{1,0:T(8,128)}), f32[128,2432]{1,0:T(8,128)}) %reduce-scatter.2.cloned.1.call-update) | async-done | bytes 1245200 | tf_op jit(solution)/shard_map/reduce_scatter | solution.py:41
  (9 shorter events, 0.0 us)
Async XLA Ops:
  6.5 73.6 %all-gather.2.cloned.1.call-start = ((), (), s32[]{:S(2)}) async-start(), calls=%async_computation.1 | async-start | bytes 3145728 | tf_op jit(solution)/shard_map/all_gather | solution.py:33
  6.5 15.1 %collective-permute-start = (bf16[128,1024]{1,0:T(8,128)(2,1)}, bf16[128,1024]{1,0:T(8,128)(2,1)S(1)}, u32[]{:S(2)}, u32[]{:S(2)}) collective-permute-start(bf16[128,1024]{1,0:T(8,128)(2,1)} %param.4), channel_id=1, source_target_pairs={{0,30},{2,0},{4,2},{6,4},{8,6},{10,8},{12,10},{14,12},{16,14},{18,... | collective-permute-start | bytes 786440 | tf_op jit(solution)/shard_map/ppermute | solution.py:11
  13.5 12.6 %collective-permute-start.2 = (bf16[128,1024]{1,0:T(8,128)(2,1)}, bf16[128,1024]{1,0:T(8,128)(2,1)S(1)}, u32[]{:S(2)}, u32[]{:S(2)}) collective-permute-start(bf16[128,1024]{1,0:T(8,128)(2,1)} %param.4), channel_id=1, source_target_pairs={{0,26},{2,28},{4,30},{6,0},{8,2},{10,4},{12,6},{14,8},{16,10},{18,... | collective-permute-start | bytes 786440 | tf_op jit(solution)/shard_map/ppermute | solution.py:11
  13.5 17.1 %collective-permute-start.1 = (bf16[128,1024]{1,0:T(8,128)(2,1)}, bf16[128,1024]{1,0:T(8,128)(2,1)S(1)}, u32[]{:S(2)}, u32[]{:S(2)}) collective-permute-start(bf16[128,1024]{1,0:T(8,128)(2,1)} %param.4), channel_id=1, source_target_pairs={{0,28},{2,30},{4,0},{6,2},{8,4},{10,6},{12,8},{14,10},{16,12},{18,... | collective-permute-start | bytes 786440 | tf_op jit(solution)/shard_map/ppermute | solution.py:11
  17.5 15.0 %copy-start = (bf16[128,2432]{1,0:T(8,128)(2,1)S(1)}, bf16[128,2432]{1,0:T(8,128)(2,1)}, u32[]{:S(2)}) copy-start(bf16[128,2432]{1,0:T(8,128)(2,1)} %param.5) | copy-start | bytes 1867780
  17.5 20.2 %copy-start.1 = (s32[16]{0:T(128)S(1)}, s32[16]{0:T(128)}, u32[]{:S(2)}) copy-start(s32[16]{0:T(128)} %param.7) | copy-start | bytes 196
  32.4 491.3 %reduce-scatter.2.cloned.1.call-start = ((), (), s32[]{:S(2)}) async-start(), calls=%async_computation.2 | async-start | bytes 21168128 | tf_op jit(solution)/shard_map/reduce_scatter | solution.py:41
  32.4 22.2 %collective-permute-start.4 = (bf16[128,2432]{1,0:T(8,128)(2,1)S(1)}, bf16[128,2432]{1,0:T(8,128)(2,1)S(1)}, u32[]{:S(2)}, u32[]{:S(2)}) collective-permute-start(bf16[128,2432]{1,0:T(8,128)(2,1)S(1)} %copy-done), channel_id=1, source_target_pairs={{0,28},{2,30},{4,0},{6,2},{8,4},{10,6},{12,8},{14,10},{16,12},{18,... | collective-permute-start | bytes 1867784 | tf_op jit(solution)/shard_map/ppermute | solution.py:11
  37.6 31.2 %collective-permute-start.3 = (bf16[128,2432]{1,0:T(8,128)(2,1)S(1)}, bf16[128,2432]{1,0:T(8,128)(2,1)S(1)}, u32[]{:S(2)}, u32[]{:S(2)}) collective-permute-start(bf16[128,2432]{1,0:T(8,128)(2,1)S(1)} %copy-done), channel_id=1, source_target_pairs={{0,30},{2,0},{4,2},{6,4},{8,6},{10,8},{12,10},{14,12},{16,14},{18,... | collective-permute-start | bytes 1867784 | tf_op jit(solution)/shard_map/ppermute | solution.py:11
  37.6 42.6 %collective-permute-start.5 = (bf16[128,2432]{1,0:T(8,128)(2,1)S(1)}, bf16[128,2432]{1,0:T(8,128)(2,1)S(1)}, u32[]{:S(2)}, u32[]{:S(2)}) collective-permute-start(bf16[128,2432]{1,0:T(8,128)(2,1)S(1)} %copy-done), channel_id=1, source_target_pairs={{0,26},{2,28},{4,30},{6,0},{8,2},{10,4},{12,6},{14,8},{16,10},{18,... | collective-permute-start | bytes 1867784 | tf_op jit(solution)/shard_map/ppermute | solution.py:11
Sparse Core Ops, SparseCore 0:
  32.5 11.3 all-gather.1
  112.9 410.7 reduce-scatter.1
where the time goes:
time: 536 us; the launch traced here: 531 us
  waiting for transfers between devices  464 us (87%)
  other arithmetic  20.2 us (4%)
  between operations  14.7 us (3%)
  matrix products  13.9 us (3%)
  starting transfers between devices  13.2 us (2%)
    reduce_scatter x1, waiting for transfers between devices, local(): lax.psum_scatter(term * (present * factor * overall), 'dp', scatter_dimen...  411 us
    ppermute x6, waiting for transfers between devices, passed_along(): lax.ppermute(value, axis, [(i, (i + by) % length) for i in range(length)])  53.2 us
    mul x1, other arithmetic, local(): term * (present * factor * overall)  14.9 us
    dot_general x1, matrix products, local(): lax.dot_general(lax.all_gather(scaled_rows, 'tensor', axis=1, tiled=True)...  13.9 us
    ppermute x6, starting transfers between devices, passed_along(): lax.ppermute(value, axis, [(i, (i + by) % length) for i in range(length)])  13.2 us
  transfers between devices with their start and end apart: 8, of which 7 were waited for; matrix products, arithmetic and copies ran while one was open for 1% of the time, Pallas kernels for 0%

commit v1 on v0

--- a/solution.py
+++ b/solution.py
@@ -1,9 +1,16 @@
+import functools
 import math
 
 import jax
 import jax.numpy as jnp
 from jax import lax
+from jax.experimental import pallas as pl
+from jax.experimental.pallas import tpu as pltpu
 from jax.sharding import PartitionSpec as P
+
+LANES = 128
+PLANE = 4
+VMEM_BUDGET = 48 * 1024 * 1024
 
 
 def passed_along(value, axis, by):
@@ -43,9 +50,441 @@
     )
 
 
+def kernel(
+    planes, slots, limit, overall, entries,
+    acts_ref, grads_ref, coding_ref, alive_ref, out_ref,
+    gbuf, xplane, xcross, xall, apart, apeer, msend, mrecv, lhs,
+    lsem, s_line, r_line, s_aline, r_aline, s_pair, r_pair, s_one, r_one,
+    s_x, r_x, s_a2a, r_a2a, s_m, r_m,
+):
+    rows, half = acts_ref.shape
+    cols = grads_ref.shape[1]
+    n = planes * PLANE
+    d = lax.axis_index("dp")
+    t = lax.axis_index("tensor")
+    z = d // PLANE
+    c = lax.rem(d, PLANE)
+    x = lax.rem(c, 2)
+    y = c // 2
+    cx = y * 2 + (1 - x)
+    cy = (1 - y) * 2 + x
+    xpeer = (z * PLANE + cx, t)
+    ypeer = (z * PLANE + cy, t)
+    other = (d, 1 - t)
+    top = planes - 1
+
+    def at_plane(plane):
+        return (plane * PLANE + c, t)
+
+    tiles = cols // LANES
+    na = max(1, (tiles * 2 + 10) // 19)
+    nb = (tiles - 2 * na + 1) // 2
+    ga = (0, na * LANES)
+    gd = (na * LANES, na * LANES)
+    gad = (0, 2 * na * LANES)
+    gb = (2 * na * LANES, nb * LANES)
+    gc = ((2 * na + nb) * LANES, cols - (2 * na + nb) * LANES)
+    gbc = (2 * na * LANES, cols - 2 * na * LANES)
+
+    def g(slot, count, group):
+        start = slot * rows
+        return gbuf.at[pl.ds(pl.multiple_of(start, rows), rows * count), pl.ds(*group)]
+
+    def remote(ref, dst, send, recv, peer):
+        return pltpu.make_async_remote_copy(
+            src_ref=ref, dst_ref=dst, send_sem=send, recv_sem=recv,
+            device_id=peer, device_id_type=pl.DeviceIdType.MESH,
+        )
+
+    loads = [
+        pltpu.make_async_copy(grads_ref, g(d, 1, (0, cols)), lsem.at[0]),
+        pltpu.make_async_copy(
+            acts_ref, xplane.at[pl.ds(pl.multiple_of(c * rows, rows), rows), :], lsem.at[1]
+        ),
+    ]
+    for load in loads:
+        load.start()
+    barrier = pltpu.get_barrier_semaphore()
+
+    def greet(peer):
+        pl.semaphore_signal(barrier, inc=1, device_id=peer, device_id_type=pl.DeviceIdType.MESH)
+
+    for peer in (xpeer, ypeer, other):
+        greet(peer)
+    for step in range(1, planes):
+        greet(at_plane(lax.rem(z + step, planes)))
+    pl.semaphore_wait(barrier, 2 + planes)
+    for load in loads:
+        load.wait()
+
+    def line(plane, up):
+        peer = at_plane(jnp.minimum(z + 1, top) if up else jnp.maximum(z - 1, 0))
+        ref = g(plane * PLANE + c, 1, gbc)
+        return remote(ref, ref, s_line.at[int(up), plane], r_line.at[plane], peer)
+
+    def aline(plane, up):
+        peer = at_plane(jnp.minimum(z + 1, top) if up else jnp.maximum(z - 1, 0))
+        ref = g(plane * PLANE, PLANE, gad)
+        return remote(ref, ref, s_aline.at[int(up), plane], r_aline.at[plane], peer)
+
+    def pair(kind, plane):
+        slot, group, peer = {
+            0: (c, gb, ypeer),
+            1: (c, gc, xpeer),
+            2: (c, gb, xpeer),
+            3: (cy, gb, xpeer),
+            4: (c, gc, ypeer),
+            5: (cx, gc, ypeer),
+        }[kind]
+        ref = g(plane * PLANE + slot, 1, group)
+        return remote(ref, ref, s_pair.at[kind, plane], r_pair.at[kind, plane], peer)
+
+    def one(kind):
+        slot, count, group, peer = {
+            0: (c, 1, ga, xpeer),
+            1: (c, 1, gd, ypeer),
+            2: (y * 2, 2, ga, ypeer),
+            3: (c, 1, gd, xpeer),
+            4: (cy, 1, gd, xpeer),
+        }[kind]
+        ref = g(z * PLANE + slot, count, group)
+        return remote(ref, ref, s_one.at[kind], r_one.at[kind], peer)
+
+    def xrows(slot, part=None):
+        if part is None:
+            return xplane.at[pl.ds(pl.multiple_of(slot * rows, rows), rows), :]
+        size = rows // 2
+        return xplane.at[pl.ds(pl.multiple_of(slot * rows + part * size, size), size), :]
+
+    def xcopy(kind):
+        ref, dst, peer = {
+            0: (xrows(c), xrows(c), xpeer),
+            1: (xrows(c), xrows(c), ypeer),
+            2: (xrows(cx, 0), xrows(cx, 0), ypeer),
+            3: (xrows(cy, 1), xrows(cy, 1), xpeer),
+            4: (xrows(c), xcross, at_plane(lax.rem(z + top, planes))),
+        }[kind]
+        return remote(ref, dst, s_x.at[kind], r_x.at[kind], peer)
+
+    def in_line(plane, sign, action):
+        ok = (plane >= 0) if sign < 0 else (plane <= top)
+
+        @pl.when(ok)
+        def _():
+            action(plane)
+
+    def both(step, action):
+        in_line(z - 1 - step, -1, functools.partial(action, up=True))
+        in_line(z + 1 + step, 1, functools.partial(action, up=False))
+
+    def forward(make, plane, up):
+        @pl.when((z < top) if up else (z > 0))
+        def _():
+            make(plane, up).start()
+
+    def start_pairs(kinds, plane):
+        for kind in kinds:
+            pair(kind, plane).start()
+
+    one(0).start()
+    one(1).start()
+    for up in (True, False):
+        forward(line, z, up)
+    pair(1, z).start()
+    pair(0, z).start()
+    one(0).wait_recv()
+    one(2).start()
+    one(1).wait_recv()
+    one(3).start()
+    one(4).start()
+    xcopy(0).start()
+    xcopy(1).start()
+    start_pairs((2, 4), z)
+    for kind in (2, 3, 4):
+        one(kind).wait_recv()
+    for up in (True, False):
+        forward(aline, z, up)
+    xcopy(4).start()
+    pair(1, z).wait_recv()
+    pair(5, z).start()
+    pair(0, z).wait_recv()
+    pair(3, z).start()
+
+    def line_arrived(plane, up):
+        line(plane, up).wait_recv()
+        forward(line, plane, up)
+        start_pairs((0, 1, 2, 4), plane)
+
+    def aline_arrived(plane, up):
+        aline(plane, up).wait_recv()
+        forward(aline, plane, up)
+
+    def second(plane, up):
+        pair(1, plane).wait_recv()
+        pair(5, plane).start()
+        pair(0, plane).wait_recv()
+        pair(3, plane).start()
+
+    both(0, line_arrived)
+    xcopy(0).wait_recv()
+    xcopy(2).start()
+    xcopy(1).wait_recv()
+    xcopy(3).start()
+    both(0, aline_arrived)
+    xcopy(2).wait_recv()
+    xcopy(3).wait_recv()
+
+    feats = xall.shape[1]
+    per = half // (PLANE * feats)
+    holder = z // per
+
+    def share(plane):
+        offset = (plane - t * per) * PLANE * feats + c * feats
+        src = xplane.at[:, pl.ds(pl.multiple_of(offset, feats), feats)]
+        dst = xall.at[pl.ds(pl.multiple_of(z * PLANE * rows, rows), PLANE * rows), :]
+        return src, dst
+
+    def a2a(plane, source):
+        src, dst = share(plane)
+        return remote(src, dst, s_a2a.at[plane], r_a2a.at[source], at_plane(plane))
+
+    def local_share():
+        src, dst = share(z)
+        return pltpu.make_async_copy(src, dst, lsem.at[2])
+
+    for plane in range(planes):
+        @pl.when((plane // per == t) & (plane != z))
+        def _(plane=plane):
+            a2a(plane, z).start()
+
+    @pl.when(holder == t)
+    def _():
+        local_share().start()
+
+    xcopy(4).wait_recv()
+    dims = (((1,), (1,)), ((), ()))
+    own_x = xplane[pl.ds(pl.multiple_of(c * rows, rows), rows), :]
+    apart[:rows, :] = lax.dot_general(own_x, xplane[...], dims, preferred_element_type=jnp.float32)
+    apart[rows:, :] = lax.dot_general(
+        xcross[...], xplane[...], dims, preferred_element_type=jnp.float32
+    )
+
+    both(0, second)
+    both(1, line_arrived)
+    both(1, aline_arrived)
+    exchange = remote(apart, apeer, s_one.at[5], r_one.at[5], other)
+    exchange.start()
+    both(2, line_arrived)
+    both(1, second)
+
+    whole = remote(xall, xall, s_one.at[6], r_one.at[6], other)
+
+    @pl.when(holder == t)
+    def _():
+        for step in range(1, planes):
+            a2a(z, lax.rem(z + step, planes)).wait_recv()
+        local_share().wait()
+        whole.start()
+
+    @pl.when(holder != t)
+    def _():
+        whole.wait_recv()
+
+    both(2, second)
+
+    exchange.wait()
+    apart[...] = apart[...] + apeer[...]
+    row = lax.broadcasted_iota(jnp.int32, (n, LANES), 0)
+    lane = lax.broadcasted_iota(jnp.int32, (n, LANES), 1)
+    coefs = jnp.zeros((n, LANES), jnp.float32)
+    for slot in range(slots):
+        coefs = coefs + jnp.where(
+            lane == lax.rem(row + slot, n), coding_ref[:, slot : slot + 1].astype(jnp.float32), 0.0
+        )
+
+    both(2, aline_arrived)
+    for plane in range(planes):
+        for kind in (2, 3, 4, 5):
+            pair(kind, plane).wait_recv()
+
+    def products(slot, base):
+        block = gbuf[pl.ds(pl.multiple_of(slot * rows, rows), rows), :]
+        plane_rows = gbuf[pl.ds(pl.multiple_of(z * PLANE * rows, rows), PLANE * rows), :]
+        grams = lax.dot_general(block, plane_rows, dims, preferred_element_type=jnp.float32)
+        sums = jnp.sum(grams * apart[base : base + rows, :], axis=0, keepdims=True)
+        return [
+            jnp.sum(sums[:, k * rows : (k + 1) * rows], axis=1, keepdims=True) for k in range(PLANE)
+        ]
+
+    ahead = lax.rem(z + 1, planes) * PLANE + c
+    total = jnp.zeros((n, LANES), jnp.float32)
+    for k, value in enumerate(products(d, 0)):
+        total = total + jnp.where((row == z * PLANE + k) & (lane == d), value, 0.0)
+    for k, value in enumerate(products(ahead, rows)):
+        p = z * PLANE + k
+        here = ((row == p) & (lane == ahead)) | ((row == ahead) & (lane == p))
+        total = total + jnp.where(here, value, 0.0)
+    for index, peer in enumerate((other, xpeer, ypeer)):
+        msend[index] = total
+        hop = remote(msend.at[index], mrecv.at[index], s_m.at[index], r_m.at[index], peer)
+        hop.start()
+        hop.wait()
+        total = total + mrecv[index]
+    msend[3] = total
+    hops = []
+    for step in range(1, planes):
+        hops.append(
+            remote(
+                msend.at[3], mrecv.at[2 + step], s_m.at[2 + step], r_m.at[2 + step],
+                at_plane(lax.rem(z + step, planes)),
+            )
+        )
+        hops[-1].start()
+    for hop in hops:
+        hop.wait()
+    for step in range(1, planes):
+        total = total + mrecv[2 + step]
+
+    spread = jnp.zeros((n, LANES), jnp.float32)
+    for p in range(n):
+        spread = spread + coefs[:, p : p + 1] * total[p : p + 1, :]
+    squares = jnp.sum(spread * coefs, axis=1, keepdims=True)
+    factor = jnp.minimum(1.0, limit / jnp.sqrt(squares / entries + 1e-06))
+    scaled = alive_ref[...].astype(jnp.float32) * factor * overall
+    weights = jnp.sum(scaled * coefs, axis=0, keepdims=True)
+
+    for p in range(n):
+        block = jnp.transpose(xall[p * rows : (p + 1) * rows, :].astype(jnp.float32))
+        block = block * weights[:, p : p + 1]
+        high = block.astype(jnp.bfloat16)
+        lhs[:feats, p * rows : (p + 1) * rows] = high
+        lhs[feats:, p * rows : (p + 1) * rows] = (block - high.astype(jnp.float32)).astype(
+            jnp.bfloat16
+        )
+
+    def write(start, size):
+        both_parts = jnp.dot(
+            lhs[...], gbuf[:, pl.ds(start, size)], preferred_element_type=jnp.float32
+        )
+        out_ref[:, pl.ds(start, size)] = both_parts[:feats] + both_parts[feats:]
+
+    wide = 2 * LANES
+
+    @pl.loop(0, cols // wide)
+    def _(tile):
+        write(pl.multiple_of(tile * wide, wide), wide)
+
+    if cols % wide:
+        write(cols - cols % wide, cols % wide)
+
+    for kind in range(5):
+        one(kind).wait_send()
+        xcopy(kind).wait_send()
+    for plane in range(planes):
+        for kind in range(6):
+            pair(kind, plane).wait_send()
+
+        @pl.when((plane // per == t) & (plane != z))
+        def _(plane=plane):
+            a2a(plane, z).wait_send()
+
+        @pl.when((plane <= z) & (z < top))
+        def _(plane=plane):
+            line(plane, True).wait_send()
+            aline(plane, True).wait_send()
+
+        @pl.when((plane >= z) & (z > 0))
+        def _(plane=plane):
+            line(plane, False).wait_send()
+            aline(plane, False).wait_send()
+
+    @pl.when(holder == t)
+    def _():
+        whole.wait_send()
+
+
+def gathered(activations, dgrad, coding, alive):
+    workers = lax.axis_size("dp")
+    rows, half = activations.shape
+    cols = dgrad.shape[1]
+    tensor = lax.axis_size("tensor")
+    planes = workers // PLANE
+    feats = half * tensor // workers
+    limit = 8.0 * math.sqrt(rows)
+    overall = 1.0 / (limit * math.sqrt(workers))
+    body = functools.partial(
+        kernel, planes, coding.shape[1], limit, overall, float(half * tensor * cols * tensor)
+    )
+    dma = pltpu.SemaphoreType.DMA
+    vmem = pl.BlockSpec(memory_space=pltpu.VMEM)
+    return pl.pallas_call(
+        body,
+        out_shape=jax.ShapeDtypeStruct((feats, cols), jnp.float32),
+        in_specs=[pl.BlockSpec(memory_space=pl.ANY)] * 2 + [vmem] * 2,
+        out_specs=vmem,
+        scratch_shapes=[
+            pltpu.VMEM((workers * rows, cols), jnp.bfloat16),
+            pltpu.VMEM((PLANE * rows, half), jnp.bfloat16),
+            pltpu.VMEM((rows, half), jnp.bfloat16),
+            pltpu.VMEM((workers * rows, feats), jnp.bfloat16),
+            pltpu.VMEM((2 * rows, PLANE * rows), jnp.float32),
+            pltpu.VMEM((2 * rows, PLANE * rows), jnp.float32),
+            pltpu.VMEM((4, workers, LANES), jnp.float32),
+            pltpu.VMEM((2 + planes, workers, LANES), jnp.float32),
+            pltpu.VMEM((2 * feats, workers * rows), jnp.bfloat16),
+            dma((3,)),
+            dma((2, planes)),
+            dma((planes,)),
+            dma((2, planes)),
+            dma((planes,)),
+            dma((6, planes)),
+            dma((6, planes)),
+            dma((7,)),
+            dma((7,)),
+            dma((5,)),
+            dma((5,)),
+            dma((planes,)),
+            dma((planes,)),
+            dma((2 + planes,)),
+            dma((2 + planes,)),
+        ],
+        compiler_params=pltpu.CompilerParams(
+            collective_id=0, has_side_effects=True, vmem_limit_bytes=VMEM_BUDGET
+        ),
+    )(activations, dgrad, coding, alive.reshape(workers, 1))
+
+
+def fits(activations, dgrad, coding):
+    workers = lax.axis_size("dp")
+    rows, half = activations.shape
+    cols = dgrad.shape[1]
+    tensor = lax.axis_size("tensor")
+    width = half * tensor
+    planes = workers // PLANE
+    return (
+        tensor == 2
+        and workers % PLANE == 0
+        and PLANE <= workers <= LANES
+        and planes >= 3
+        and planes % tensor == 0
+        and coding.shape[1] <= PLANE
+        and rows == LANES
+        and width == workers * LANES
+        and cols % LANES == 0
+        and cols >= 8 * LANES
+        and workers * rows * cols * 2 <= VMEM_BUDGET // 2
+    )
+
+
+def step(activations, dgrad, coding, alive):
+    if fits(activations, dgrad, coding):
+        return gathered(activations, dgrad, coding, alive)
+    return local(activations, dgrad, coding, alive)
+
+
 def solution(mesh):
     return jax.shard_map(
-        local,
+        step,
         mesh=mesh,
         in_specs=(P("dp", "tensor"), P("dp", "tensor"), P(), P()),
         out_specs=P("dp", "tensor"),

time: 536 us -> 116 us (0.22)
  waiting for transfers between devices: 464 us -> 0 us
  Pallas kernels: 0 us -> 111 us
  other arithmetic: 20.2 us -> 0 us
  between operations: 14.7 us -> 0.01 us
  matrix products: 13.9 us -> 0 us
  starting transfers between devices: 13.2 us -> 0 us
    reduce_scatter x1 -> x0, waiting for transfers between devices: 411 us -> none  [local(): lax.psum_scatter(term * (present * factor * overall), 'dp', scatter_dimen...]
    pallas_call x0 -> x1, Pallas kernels: none -> 111 us  [gathered(): pl.pallas_call(body, out_shape=jax.ShapeDtypeStruct((feats, cols), jnp.fl...]
    ppermute x6 -> x0, waiting for transfers between devices: 53.2 us -> none  [passed_along(): lax.ppermute(value, axis, [(i, (i + by) % length) for i in range(length)])]
    mul x5 -> x0, other arithmetic: 18.4 us -> none  [the longest x1 14.9 us: local(): term * (present * factor * overall)]
    dot_general x1 -> x0, matrix products: 13.9 us -> none  [local(): lax.dot_general(lax.all_gather(scaled_rows, 'tensor', axis=1, tiled=True)...]
    ppermute x6 -> x0, starting transfers between devices: 13.2 us -> none  [passed_along(): lax.ppermute(value, axis, [(i, (i + by) % length) for i in range(length)])]
  transfers between devices with their start and end apart: 8 -> 0, of which waited for: 7 -> 0; matrix products, arithmetic and copies ran while one was open for 1% -> 0% of each run, Pallas kernels for 0% -> 0%
where the time goes in v1:
time: 116 us
  Pallas kernels  111 us (96%)
  local copies, waits for them, and re-layouts  4.55 us (4%)
    pallas_call x1, Pallas kernels, gathered(): pl.pallas_call(body, out_shape=jax.ShapeDtypeStruct((feats, cols), jnp.fl...  111 us
    unnamed x6, local copies, waits for them, and re-layouts  3.82 us

profile of v1, /device:TPU:0, one launch (start us, length us, event | category | flops | bytes accessed | tf_op | source)
XLA Modules:
  0.0 115.8 jit_solution(9151691998676927684)
XLA Ops:
  0.0 0.8 copy.5.coding_ref
  0.8 0.7 copy.6.alive_ref
  1.5 0.0 copy-start
  1.5 1.1 copy-done
  2.6 0.0 copy-start.1
  2.6 0.9 copy-done.1
  3.5 111.3 %shard_map.46 = f32[128,2432]{1,0:T(8,128)S(1)} custom-call(bf16[128,1024]{1,0:T(8,128)(2,1)S(1)} %copy-done.1, bf16[128,2432]{1,0:T(8,128)(2,1)S(1)} %copy-done, s32[16,4]{1,0:T(8,128)S(1)} %copy.5.coding_ref, s32[16,1]{1,0:T(8,128)S(1)} %copy.6.alive_ref), custom_call_target="tpu_custom_call" | custom-call | tf_op jit(solution)/shard_map/pallas_call | solution.py:420
  114.8 1.0 copy.8
Async XLA Ops:
  1.5 1.1 copy-start
  2.6 0.9 copy-start.1

commit v2 on v1

--- a/solution.py
+++ b/solution.py
@@ -70,6 +70,7 @@
     cy = (1 - y) * 2 + x
     xpeer = (z * PLANE + cx, t)
     ypeer = (z * PLANE + cy, t)
+    diagonal = (z * PLANE + PLANE - 1 - c, t)
     other = (d, 1 - t)
     top = planes - 1
 
@@ -109,11 +110,10 @@
     def greet(peer):
         pl.semaphore_signal(barrier, inc=1, device_id=peer, device_id_type=pl.DeviceIdType.MESH)
 
-    for peer in (xpeer, ypeer, other):
+    others = [at_plane(lax.rem(z + step, planes)) for step in range(1, planes)]
+    for peer in (xpeer, ypeer, diagonal, other, *others):
         greet(peer)
-    for step in range(1, planes):
-        greet(at_plane(lax.rem(z + step, planes)))
-    pl.semaphore_wait(barrier, 2 + planes)
+    pl.semaphore_wait(barrier, 3 + planes)
     for load in loads:
         load.wait()
 
@@ -252,15 +252,6 @@
         src, dst = share(z)
         return pltpu.make_async_copy(src, dst, lsem.at[2])
 
-    for plane in range(planes):
-        @pl.when((plane // per == t) & (plane != z))
-        def _(plane=plane):
-            a2a(plane, z).start()
-
-    @pl.when(holder == t)
-    def _():
-        local_share().start()
-
     xcopy(4).wait_recv()
     dims = (((1,), (1,)), ((), ()))
     own_x = xplane[pl.ds(pl.multiple_of(c * rows, rows), rows), :]
@@ -271,11 +262,20 @@
 
     both(0, second)
     both(1, line_arrived)
+    for plane in range(planes):
+        @pl.when((plane // per == t) & (plane != z))
+        def _(plane=plane):
+            a2a(plane, z).start()
+
+    @pl.when(holder == t)
+    def _():
+        local_share().start()
+
     both(1, aline_arrived)
     exchange = remote(apart, apeer, s_one.at[5], r_one.at[5], other)
     exchange.start()
+    both(1, second)
     both(2, line_arrived)
-    both(1, second)
 
     whole = remote(xall, xall, s_one.at[6], r_one.at[6], other)
 
@@ -324,26 +324,21 @@
         p = z * PLANE + k
         here = ((row == p) & (lane == ahead)) | ((row == ahead) & (lane == p))
         total = total + jnp.where(here, value, 0.0)
-    for index, peer in enumerate((other, xpeer, ypeer)):
-        msend[index] = total
-        hop = remote(msend.at[index], mrecv.at[index], s_m.at[index], r_m.at[index], peer)
-        hop.start()
-        hop.wait()
-        total = total + mrecv[index]
-    msend[3] = total
-    hops = []
-    for step in range(1, planes):
-        hops.append(
-            remote(
-                msend.at[3], mrecv.at[2 + step], s_m.at[2 + step], r_m.at[2 + step],
-                at_plane(lax.rem(z + step, planes)),
-            )
-        )
-        hops[-1].start()
-    for hop in hops:
-        hop.wait()
-    for step in range(1, planes):
-        total = total + mrecv[2 + step]
+    stages = ((other,), (diagonal, xpeer, ypeer), tuple(others))
+    first = 0
+    for stage, peers in enumerate(stages):
+        msend[stage] = total
+        hops = [
+            remote(msend.at[stage], mrecv.at[first + k], s_m.at[first + k], r_m.at[first + k], peer)
+            for k, peer in enumerate(peers)
+        ]
+        for hop in hops:
+            hop.start()
+        for hop in hops:
+            hop.wait()
+        for k in range(len(peers)):
+            total = total + mrecv[first + k]
+        first += len(peers)
 
     spread = jnp.zeros((n, LANES), jnp.float32)
     for p in range(n):
@@ -429,8 +424,8 @@
             pltpu.VMEM((workers * rows, feats), jnp.bfloat16),
             pltpu.VMEM((2 * rows, PLANE * rows), jnp.float32),
             pltpu.VMEM((2 * rows, PLANE * rows), jnp.float32),
-            pltpu.VMEM((4, workers, LANES), jnp.float32),
-            pltpu.VMEM((2 + planes, workers, LANES), jnp.float32),
+            pltpu.VMEM((3, workers, LANES), jnp.float32),
+            pltpu.VMEM((3 + planes, workers, LANES), jnp.float32),
             pltpu.VMEM((2 * feats, workers * rows), jnp.bfloat16),
             dma((3,)),
             dma((2, planes)),
@@ -445,8 +440,8 @@
             dma((5,)),
             dma((planes,)),
             dma((planes,)),
-            dma((2 + planes,)),
-            dma((2 + planes,)),
+            dma((3 + planes,)),
+            dma((3 + planes,)),
         ],
         compiler_params=pltpu.CompilerParams(
             collective_id=0, has_side_effects=True, vmem_limit_bytes=VMEM_BUDGET

time: 116 us -> 107 us (0.922)
  Pallas kernels: 111 us -> 102 us
    pallas_call x1, Pallas kernels: 111 us -> 102 us  [gathered(): pl.pallas_call(body, out_shape=jax.ShapeDtypeStruct((feats, cols), jnp.fl...]
where the time goes in v2:
time: 107 us
  Pallas kernels  102 us (95%)
  local copies, waits for them, and re-layouts  4.55 us (4%)
    pallas_call x1, Pallas kernels, gathered(): pl.pallas_call(body, out_shape=jax.ShapeDtypeStruct((feats, cols), jnp.fl...  102 us
    unnamed x6, local copies, waits for them, and re-layouts  3.82 us

profile of v2, /device:TPU:0, one launch (start us, length us, event | category | flops | bytes accessed | tf_op | source)
XLA Modules:
  0.0 107.0 jit_solution(2237715539706583456)
XLA Ops:
  0.0 0.8 copy.5.coding_ref
  0.8 0.7 copy.6.alive_ref
  1.5 0.0 copy-start
  1.5 1.1 %copy-done = bf16[128,2432]{1,0:T(8,128)(2,1)S(1)} copy-done((bf16[128,2432]{1,0:T(8,128)(2,1)S(1)}, bf16[128,2432]{1,0:T(8,128)(2,1)}, u32[]{:S(2)}) %copy-start) | copy-done | bytes 622616
  2.6 0.0 copy-start.1
  2.6 0.9 copy-done.1
  3.5 102.4 %shard_map.46 = f32[128,2432]{1,0:T(8,128)S(1)} custom-call(bf16[128,1024]{1,0:T(8,128)(2,1)S(1)} %copy-done.1, bf16[128,2432]{1,0:T(8,128)(2,1)S(1)} %copy-done, s32[16,4]{1,0:T(8,128)S(1)} %copy.5.coding_ref, s32[16,1]{1,0:T(8,128)S(1)} %copy.6.alive_ref), custom_call_target="tpu_custom_call" | custom-call | tf_op jit(solution)/shard_map/pallas_call | solution.py:415
  106.0 1.0 copy.8
Async XLA Ops:
  1.5 1.1 %copy-start = (bf16[128,2432]{1,0:T(8,128)(2,1)S(1)}, bf16[128,2432]{1,0:T(8,128)(2,1)}, u32[]{:S(2)}) copy-start(bf16[128,2432]{1,0:T(8,128)(2,1)} %grads_ref.1) | copy-start | bytes 1867780
  2.6 0.9 copy-start.1

commit v3 on v2

--- a/solution.py
+++ b/solution.py
@@ -302,6 +302,10 @@
             lane == lax.rem(row + slot, n), coding_ref[:, slot : slot + 1].astype(jnp.float32), 0.0
         )
 
+    for p in range(n):
+        turned = jnp.transpose(xall[p * rows : (p + 1) * rows, :].astype(jnp.float32))
+        lhs[:feats, p * rows : (p + 1) * rows] = turned.astype(jnp.bfloat16)
+
     both(2, aline_arrived)
     for plane in range(planes):
         for kind in (2, 3, 4, 5):
@@ -349,7 +353,7 @@
     weights = jnp.sum(scaled * coefs, axis=0, keepdims=True)
 
     for p in range(n):
-        block = jnp.transpose(xall[p * rows : (p + 1) * rows, :].astype(jnp.float32))
+        block = lhs[:feats, p * rows : (p + 1) * rows].astype(jnp.float32)
         block = block * weights[:, p : p + 1]
         high = block.astype(jnp.bfloat16)
         lhs[:feats, p * rows : (p + 1) * rows] = high

time: 107 us -> 107 us (level)
  no operation moved by 1% of the time
where the time goes in v3:
time: 107 us
  Pallas kernels  102 us (95%)
  local copies, waits for them, and re-layouts  4.55 us (4%)
    pallas_call x1, Pallas kernels, gathered(): pl.pallas_call(body, out_shape=jax.ShapeDtypeStruct((feats, cols), jnp.fl...  102 us
    unnamed x6, local copies, waits for them, and re-layouts  3.82 us

profile of v3, /device:TPU:0, one launch (start us, length us, event | category | flops | bytes accessed | tf_op | source)
XLA Modules:
  0.0 106.9 jit_solution(13748828995626350532)
XLA Ops:
  0.0 0.8 copy.5.coding_ref
  0.8 0.7 copy.6.alive_ref
  1.5 0.0 copy-start
  1.5 1.1 %copy-done = bf16[128,2432]{1,0:T(8,128)(2,1)S(1)} copy-done((bf16[128,2432]{1,0:T(8,128)(2,1)S(1)}, bf16[128,2432]{1,0:T(8,128)(2,1)}, u32[]{:S(2)}) %copy-start) | copy-done | bytes 622616
  2.6 0.0 copy-start.1
  2.6 0.9 copy-done.1
  3.5 102.3 %shard_map.46 = f32[128,2432]{1,0:T(8,128)S(1)} custom-call(bf16[128,1024]{1,0:T(8,128)(2,1)S(1)} %copy-done.1, bf16[128,2432]{1,0:T(8,128)(2,1)S(1)} %copy-done, s32[16,4]{1,0:T(8,128)S(1)} %copy.5.coding_ref, s32[16,1]{1,0:T(8,128)S(1)} %copy.6.alive_ref), custom_call_target="tpu_custom_call" | custom-call | tf_op jit(solution)/shard_map/pallas_call | solution.py:419
  105.9 1.0 copy.8
Async XLA Ops:
  1.5 1.1 %copy-start = (bf16[128,2432]{1,0:T(8,128)(2,1)S(1)}, bf16[128,2432]{1,0:T(8,128)(2,1)}, u32[]{:S(2)}) copy-start(bf16[128,2432]{1,0:T(8,128)(2,1)} %grads_ref.1) | copy-start | bytes 1867780
  2.6 0.9 copy-start.1
